TPU v7x, 256 devices: a whole 4x4x8 slice. The times are simulated.
256 devices in a mesh: src: 16 (over z, core), tgt: 16 (over y, x).
Axes of the slice: x: 4, y: 4, z: 8, core: 2. Of those that a mesh axis runs over, the one named last changes fastest.
Arguments:
- source: float32 [32, 16384], P(None, ('src', 'tgt')), may hold values from -2 to 2
- target: float32 [32, 26624], P(None, ('tgt', 'src')), may hold values from -2 to 2
- target_pot: float32 [26624], P(('tgt', 'src')), may hold values from -1 to 8
- source_logw: float32 [16384], P(('src', 'tgt')), may hold values from -14 to -9
- target_logw: float32 [26624], P(('tgt', 'src')), may hold values from -14 to -9
Outputs:
- f_new: float32 [16384], P(('src', 'tgt'))
- g_new: float32 [26624], P(('tgt', 'src'))
- projection: float32 [32, 16384], P(None, ('src', 'tgt'))
All inputs are finite; a program needn't handle non-finite values.
Results may differ from a plain program's by a relative error of at most 0.0003.
Values sent between devices are 32-bit elements; how exact they have to be, the bound alone decides.
A program may use at most 64 MiB of HBM per device.

v0:
```python
import math
import jax
import jax.numpy as jnp
from jax import lax
from jax.sharding import PartitionSpec as P

EPSILON = 0.05
HIGHEST = lax.Precision.HIGHEST


def cost_scores(row_cells, col_cells, col_sq, col_pot, col_logw):
    cross_term = lax.dot_general(
        row_cells,
        col_cells,
        (((0,), (0,)), ((), ())),
        precision=HIGHEST,
        preferred_element_type=jnp.float32,
    )
    cost_tile = jnp.sum(row_cells * row_cells, 0)[:, None] + col_sq[None, :] - 2.0 * cross_term
    return (col_pot[None, :] - cost_tile) / EPSILON + col_logw[None, :]


def log_sums(row_cells, col_cells, col_pot, col_logw, weighted):
    feat_dim, row_count = row_cells.shape
    row_block = math.gcd(row_count, 512)
    col_sq = jnp.sum(col_cells * col_cells, 0)
    blocks = row_cells.reshape(feat_dim, row_count // row_block, row_block).transpose(1, 0, 2)

    def one_block(cells_block):
        scores = cost_scores(cells_block, col_cells, col_sq, col_pot, col_logw)
        row_top = jnp.max(scores, 1)
        kernel = jnp.exp(scores - row_top[:, None])
        totals = jnp.sum(kernel, 1)
        if weighted:
            moments = lax.dot_general(
                col_cells,
                kernel,
                (((1,), (1,)), ((), ())),
                precision=HIGHEST,
                preferred_element_type=jnp.float32,
            )
            return (row_top, totals, moments)
        return (row_top, totals)

    result = lax.map(one_block, blocks)
    row_top = result[0].reshape(row_count)
    totals = result[1].reshape(row_count)
    if weighted:
        moments = result[2].transpose(1, 0, 2).reshape(feat_dim, row_count)
        return (row_top, totals, moments)
    return (row_top, totals)


def body(source, target, target_pot, source_logw, target_logw):
    src_cells, src_logw = (
        lax.all_gather(source, "tgt", axis=1, tiled=True),
        lax.all_gather(source_logw, "tgt", axis=0, tiled=True),
    )
    tgt_cells, tgt_pot, tgt_logw = (
        lax.all_gather(target, "src", axis=1, tiled=True),
        lax.all_gather(target_pot, "src", axis=0, tiled=True),
        lax.all_gather(target_logw, "src", axis=0, tiled=True),
    )
    row_top, row_totals = log_sums(src_cells, tgt_cells, tgt_pot, tgt_logw, False)
    highest = lax.pmax(row_top, "tgt")
    row_totals = lax.psum(row_totals * jnp.exp(row_top - highest), "tgt")
    row_top = highest
    f_block = -EPSILON * (row_top + jnp.log(row_totals))
    col_top, col_totals = log_sums(tgt_cells, src_cells, f_block, src_logw, False)
    col_highest = lax.pmax(col_top, "src")
    col_totals = lax.psum(col_totals * jnp.exp(col_top - col_highest), "src")
    col_top = col_highest
    g_block = -EPSILON * (col_top + jnp.log(col_totals))
    mine_rows = source.shape[1]
    mine_cols = target.shape[1]
    f_new = lax.dynamic_slice_in_dim(f_block, lax.axis_index("tgt") * mine_rows, mine_rows)
    g_new = lax.dynamic_slice_in_dim(g_block, lax.axis_index("src") * mine_cols, mine_cols)
    proj_top, proj_totals, moments = log_sums(src_cells, tgt_cells, g_block, tgt_logw, True)
    proj_highest = lax.pmax(proj_top, "tgt")
    rescale = jnp.exp(proj_top - proj_highest)
    moments_mine, totals_mine = (
        lax.psum_scatter(moments * rescale[None, :], "tgt", scatter_dimension=1, tiled=True),
        lax.psum_scatter(proj_totals * rescale, "tgt", scatter_dimension=0, tiled=True),
    )
    projection = moments_mine / totals_mine[None, :]
    return (f_new, g_new, projection)


def solution(mesh):
    return jax.shard_map(
        body,
        mesh=mesh,
        in_specs=(
            P(None, ("src", "tgt")),
            P(None, ("tgt", "src")),
            P(("tgt", "src")),
            P(("src", "tgt")),
            P(("tgt", "src")),
        ),
        out_specs=(P(("src", "tgt")), P(("tgt", "src")), P(None, ("src", "tgt"))),
        check_vma=False,
    )
```

profile of v0, /device:TPU:2, one launch (start us, length us, event | category | flops | bytes accessed | tf_op | source)
XLA Modules:
  0.0 446.6 jit_solution(15336664736178391552)
XLA Ops:
  7.3 23.8 %all-gather = f32[16,64,32]{1,2,0:T(8,128)S(1)} all-gather(f32[1,64,32]{1,2,0:T(8,128)} %bitcast.127), channel_id=1, replica_groups=mesh['src'=16,'tgt'=16] {'tgt'}, dimensions={0}, use_global_device_ids=true | all-gather | bytes 139264 | tf_op jit(solution)/shard_map/all_gather | solution.py:56
  32.1 20.9 %all-gather.1 = f32[16,104,32]{1,2,0:T(8,128)S(1)} all-gather(f32[1,104,32]{1,2,0:T(8,128)} %bitcast.128), channel_id=1, replica_groups=mesh['src'=16,'tgt'=16] {'src'}, dimensions={0}, use_global_device_ids=true | all-gather | bytes 226304 | tf_op jit(solution)/shard_map/all_gather | solution.py:60
  54.1 1.6 multiply_reduce_fusion.1
  55.6 1.7 reshape.54
  59.2 45.9 %all-reduce.5 = (f32[1664]{0:T(1024)}, f32[1664]{0:T(1024)}) all-reduce(f32[1664]{0:T(1024)S(1)} %dynamic-update-slice, f32[1664]{0:T(1024)S(1)} %dynamic-update-slice.1), channel_id=1, replica_groups=mesh['src'=16,'tgt'=16] {'src'}, use_global_device_ids=true, to_apply=%add | all-reduce | flops 3328 | bytes 26624
  106.3 15.7 %while.38 = (s32[]{:T(128)}, f32[2,512]{1,0:T(2,128)}, f32[2,512]{1,0:T(2,128)}, f32[1664]{0:T(1024)}, f32[2,32,512]{2,1,0:T(8,128)S(1)}, /*index=5*/f32[1664]{0...) while((s32[]{:T(128)}, f32[2,512]{1,0:T(2,128)}, f32[2,512]{1,0:T(2,128)}, ...), condition=%wide.region_5.6_spmd, body=%wide.region_1.5_spmd.sunk | while | flops 334854656 | bytes 7198333 | solution.py:45
  106.3 4.6 %fusion.41 = (f32[512]{0:T(512)S(1)}, f32[512,1664]{1,0:T(8,128)S(1)}) fusion(f32[1664]{0:T(1024)} %get-tuple-element.476, f32[32,1664]{1,0:T(8,128)} %get-tuple-element.475, f32[2,32,512]{2,1,0:T(8,128)S(1)} %get-tuple-element.473, s32[]{:T(128)S(6)} %copy.48, f32[1664]{0:T(1024)} %get-tuple-element.474, f32[512]{0:T(512)S(1)} %fusion.40, ...), kind=kOutput, calls=%fused_computation.37.clone.1 | convolution fusion | flops 333118976 | bytes 3710468 | tf_op jit(solution)/shard_map/while/body/eval_jaxpr/dot_general | solution.py:12
  110.9 1.3 dynamic_update_slice.32
  112.8 1.3 dynamic_update_slice.33
  114.2 4.6 %fusion.41 = (f32[512]{0:T(512)S(1)}, f32[512,1664]{1,0:T(8,128)S(1)}) fusion(f32[1664]{0:T(1024)} %get-tuple-element.476, f32[32,1664]{1,0:T(8,128)} %get-tuple-element.475, f32[2,32,512]{2,1,0:T(8,128)S(1)} %get-tuple-element.473, s32[]{:T(128)S(6)} %copy.48, f32[1664]{0:T(1024)} %get-tuple-element.474, f32[512]{0:T(512)S(1)} %fusion.40, ...), kind=kOutput, calls=%fused_computation.37.clone.1 | convolution fusion | flops 333118976 | bytes 3710468 | tf_op jit(solution)/shard_map/while/body/eval_jaxpr/dot_general | solution.py:12
  118.8 1.3 dynamic_update_slice.32
  120.7 1.3 dynamic_update_slice.33
  122.6 36.2 %pmax.21 = f32[1024]{0:T(1024)S(1)} all-reduce(f32[1024]{0:T(1024)S(1)} %bitcast.123), channel_id=1, replica_groups=mesh['src'=16,'tgt'=16] {'tgt'}, use_global_device_ids=true, to_apply=%region_6.7 | all-reduce | flops 1024 | bytes 8192 | tf_op jit(solution)/shard_map/pmax | solution.py:65
  159.6 1.3 fusion.21
  162.4 38.6 %all-reduce.4 = (f32[1024]{0:T(1024)S(1)}, f32[1024]{0:T(1024)S(1)}) all-reduce(f32[1024]{0:T(1024)S(1)} %exponential_multiply_fusion, f32[1024]{0:T(1024)S(1)} %dynamic-update-slice.2), channel_id=1, replica_groups=mesh['src'=16,'tgt'=16] {'tgt'}, use_global_device_ids=true, to_apply=%region_7.8 | all-reduce | flops 2048 | bytes 16384 | tf_op jit(solution)/shard_map/psum | solution.py:66
  201.1 54.8 %while.39 = (s32[]{:T(128)}, f32[13,128]{1,0:T(8,128)S(1)}, f32[13,128]{1,0:T(8,128)}, f32[1024]{0:T(1024)S(1)}, f32[13,32,128]{2,0,1:T(8,128)}, /*index=5*/f32[...) while((s32[]{:T(128)}, f32[13,128]{1,0:T(8,128)S(1)}, f32[13,128]{1,0:T(8,128)}, ...), condition=%wide.region_13.14_spmd, body=%wide.region_9.13_spmd.sunk | while | flops 51519104 | bytes 1262201 | solution.py:45
  201.1 0.9 constant_dynamic-slice_fusion.2
  202.0 1.7 fusion.44
  204.0 1.3 dynamic_update_slice.35
  205.3 0.9 constant_dynamic-slice_fusion.2
  206.3 1.7 fusion.44
  208.2 1.3 dynamic_update_slice.35
  209.5 0.9 constant_dynamic-slice_fusion.2
  210.5 1.7 fusion.44
  212.4 1.3 dynamic_update_slice.35
  213.7 0.9 constant_dynamic-slice_fusion.2
  214.7 1.7 fusion.44
  216.6 1.3 dynamic_update_slice.35
  218.9 1.7 fusion.44
  220.9 1.3 dynamic_update_slice.35
  223.1 1.7 fusion.44
  225.1 1.3 dynamic_update_slice.35
  226.4 0.9 constant_dynamic-slice_fusion.2
  227.3 1.7 fusion.44
  229.3 1.3 dynamic_update_slice.35
  230.6 0.9 constant_dynamic-slice_fusion.2
  231.5 1.7 fusion.44
  233.5 1.3 dynamic_update_slice.35
  234.8 0.9 constant_dynamic-slice_fusion.2
  235.7 1.7 fusion.44
  237.7 1.3 dynamic_update_slice.35
  239.9 1.7 fusion.44
  241.9 1.3 dynamic_update_slice.35
  244.2 1.7 fusion.44
  246.1 1.3 dynamic_update_slice.35
  247.4 0.9 constant_dynamic-slice_fusion.2
  248.4 1.7 fusion.44
  250.3 1.3 dynamic_update_slice.35
  251.6 0.9 constant_dynamic-slice_fusion.2
  252.6 1.7 fusion.44
  254.5 1.3 dynamic_update_slice.35
  255.8 24.0 %pmax.22 = f32[1664]{0:T(1024)S(1)} all-reduce(f32[1664]{0:T(1024)S(1)} %bitcast.126), channel_id=1, replica_groups=mesh['src'=16,'tgt'=16] {'src'}, use_global_device_ids=true, to_apply=%region_14.15 | all-reduce | flops 1664 | bytes 13312 | tf_op jit(solution)/shard_map/pmax | solution.py:70
  280.6 24.2 %psum.15 = f32[1664]{0:T(1024)S(1)} all-reduce(f32[1664]{0:T(1024)S(1)} %bitcast_multiply_fusion.2), channel_id=1, replica_groups=mesh['src'=16,'tgt'=16] {'src'}, use_global_device_ids=true, to_apply=%region_15.16 | all-reduce | flops 1664 | bytes 13312 | tf_op jit(solution)/shard_map/psum | solution.py:71
  305.4 21.1 %while.40 = (s32[]{:T(128)}, f32[2,512]{1,0:T(2,128)S(1)}, f32[2,512]{1,0:T(2,128)S(1)}, f32[2,32,512]{2,1,0:T(8,128)}, f32[1664]{0:T(1024)}, /*index=5*/f32[2,3...) while((s32[]{:T(128)}, f32[2,512]{1,0:T(2,128)S(1)}, ...), condition=%wide.region_20.21_spmd, body=%wide.region_16.20_spmd.sunk | while | flops 662862336 | bytes 10886793 | solution.py:45
  305.5 4.6 %fusion.48 = (f32[512]{0:T(512)S(1)}, f32[512,1664]{1,0:T(8,128)S(1)}) fusion(f32[1664]{0:T(1024)} %get-tuple-element.539, f32[32,1664]{1,0:T(8,128)} %get-tuple-element.538, f32[2,32,512]{2,1,0:T(8,128)S(1)} %get-tuple-element.536, s32[]{:T(128)S(6)} %copy.68, f32[1664]{0:T(1024)} %get-tuple-element.537, f32[512]{0:T(512)S(1)} %fusion.47, ...), kind=kOutput, calls=%fused_computation.39.clone.1 | convolution fusion | flops 333118976 | bytes 3710468 | tf_op jit(solution)/shard_map/while/body/eval_jaxpr/dot_general | solution.py:12
  310.8 5.2 %fusion.50 = f32[2,32,512]{2,1,0:T(8,128)} fusion(f32[2,32,512]{2,1,0:T(8,128)} %get-tuple-element.523, s32[]{:T(128)S(6)} %copy.68, f32[32,1664]{1,0:T(8,128)} %get-tuple-element.538, f32[512,1664]{1,0:T(8,128)S(1)} %get-tuple-element.448, f32[512]{0:T(512)S(1)} %get-tuple-element.447), kind=kOutput, calls=%fused_computation.21.clone.1 | convolution fusion | flops 328007680 | bytes 3688452 | tf_op jit(solution)/shard_map/while/body/eval_jaxpr/dot_general | solution.py:35
  316.0 4.6 %fusion.48 = (f32[512]{0:T(512)S(1)}, f32[512,1664]{1,0:T(8,128)S(1)}) fusion(f32[1664]{0:T(1024)} %get-tuple-element.539, f32[32,1664]{1,0:T(8,128)} %get-tuple-element.538, f32[2,32,512]{2,1,0:T(8,128)S(1)} %get-tuple-element.536, s32[]{:T(128)S(6)} %copy.68, f32[1664]{0:T(1024)} %get-tuple-element.537, f32[512]{0:T(512)S(1)} %fusion.47, ...), kind=kOutput, calls=%fused_computation.39.clone.1 | convolution fusion | flops 333118976 | bytes 3710468 | tf_op jit(solution)/shard_map/while/body/eval_jaxpr/dot_general | solution.py:12
  321.3 5.2 %fusion.50 = f32[2,32,512]{2,1,0:T(8,128)} fusion(f32[2,32,512]{2,1,0:T(8,128)} %get-tuple-element.523, s32[]{:T(128)S(6)} %copy.68, f32[32,1664]{1,0:T(8,128)} %get-tuple-element.538, f32[512,1664]{1,0:T(8,128)S(1)} %get-tuple-element.448, f32[512]{0:T(512)S(1)} %get-tuple-element.447), kind=kOutput, calls=%fused_computation.21.clone.1 | convolution fusion | flops 328007680 | bytes 3688452 | tf_op jit(solution)/shard_map/while/body/eval_jaxpr/dot_general | solution.py:35
  327.5 35.5 %pmax.23 = f32[1024]{0:T(1024)S(1)} all-reduce(f32[1024]{0:T(1024)S(1)} %bitcast.121), channel_id=1, replica_groups=mesh['src'=16,'tgt'=16] {'tgt'}, use_global_device_ids=true, to_apply=%region_21.22 | all-reduce | flops 1024 | bytes 8192 | tf_op jit(solution)/shard_map/pmax | solution.py:79
  363.0 1.0 copy.28
  364.0 1.3 dynamic_slice.17
  365.3 1.3 dynamic_slice.18
  367.1 37.5 %all-reduce.3 = f32[1024]{0:T(1024)S(1)} all-reduce(f32[1024]{0:T(1024)S(1)} %get-tuple-element.274), channel_id=3, replica_groups=mesh['src'=16,'tgt'=16] {'tgt'}, use_global_device_ids=true, to_apply=%region_23.24.clone | all-reduce | flops 1024 | bytes 8192
  404.7 33.6 %reduce-scatter.4.cloned.1.call-done = f32[64,32]{1,0:T(8,128)} async-done(((f32[1024,32]{1,0:T(8,128)}), f32[64,32]{1,0:T(8,128)}) %reduce-scatter.4.cloned.1.call-update) | async-done | bytes 8208
  (102 shorter events, 20.6 us)
Async XLA Ops:
  7.2 50.1 %copy-start.4 = (u32[256]{0:T(256)S(1)}, u32[256]{0:T(256)}, u32[]{:S(2)}) copy-start(u32[256]{0:T(256)} %constant.89) | copy-start | bytes 3076
  7.2 51.5 %copy-start.2 = (f32[104]{0:T(128)S(1)}, f32[104]{0:T(128)}, u32[]{:S(2)}) copy-start(f32[104]{0:T(128)} %param.13) | copy-start | bytes 1252
  7.2 51.7 %copy-start.3 = (f32[104]{0:T(128)S(1)}, f32[104]{0:T(128)}, u32[]{:S(2)}) copy-start(f32[104]{0:T(128)} %param.15) | copy-start | bytes 1252
  7.2 431.1 %reduce-scatter.4.cloned.1.call-start = ((), (), s32[]{:S(2)}) async-start(), calls=%async_computation.1 | async-start | bytes 557056
  31.3 0.8 copy-start
  255.8 49.6 %copy-start.1 = (f32[1024]{0:T(1024)}, f32[1024]{0:T(1024)S(1)}, u32[]{:S(2)}) copy-start(f32[1024]{0:T(1024)S(1)} %get-tuple-element.549) | copy-start | bytes 12292
Sparse Core Ops, SparseCore 0:
  364.1 74.0 reduce-scatter.3
where the time goes:
time: 448 us; the launch traced here: 447 us
  blocking collectives  287 us (64%)
  matrix products  51 us (11%)
  local copies, waits for them, and re-layouts  49.1 us (11%)
  waiting for transfers between devices  33.6 us (8%)
  between operations  16.1 us (4%)
  other arithmetic  9.89 us (2%)
    unnamed x2, blocking collectives  83.4 us
    dot_general x17, matrix products, cost_scores(): lax.dot_general(row_cells, col_cells, (((0,), (0,)), ((), ())), precision...  40.6 us
    psum x1, blocking collectives, body(): row_totals = lax.psum(row_totals * jnp.exp(row_top - highest), 'tgt')  38.6 us
    pmax x1, blocking collectives, body(): highest = lax.pmax(row_top, 'tgt')  36.2 us
    pmax x1, blocking collectives, body(): proj_highest = lax.pmax(proj_top, 'tgt')  35.5 us
    unnamed x2, waiting for transfers between devices  33.6 us
    psum x1, blocking collectives, body(): col_totals = lax.psum(col_totals * jnp.exp(col_top - col_highest), 'src')  24.2 us
    pmax x1, blocking collectives, body(): col_highest = lax.pmax(col_top, 'src')  24 us
  transfers between devices with their start and end apart: 1, of which 1 were waited for; matrix products, arithmetic and copies ran while one was open for 1% of the time, Pallas kernels for 0%

commit v1 on v0

--- a/solution.py
+++ b/solution.py
@@ -6,6 +6,13 @@
 
 EPSILON = 0.05
 HIGHEST = lax.Precision.HIGHEST
+
+
+def all_by_exchange(x, axis, d):
+    size = lax.axis_size(axis)
+    blocks = jnp.stack([x for _ in range(size)])
+    blocks = lax.all_to_all(blocks, axis, split_axis=0, concat_axis=0)
+    return jnp.concatenate(blocks, axis=d)
 
 
 def cost_scores(row_cells, col_cells, col_sq, col_pot, col_logw):
@@ -53,7 +60,7 @@
 
 def body(source, target, target_pot, source_logw, target_logw):
     src_cells, src_logw = (
-        lax.all_gather(source, "tgt", axis=1, tiled=True),
+        all_by_exchange(source, "tgt", 1),
         lax.all_gather(source_logw, "tgt", axis=0, tiled=True),
     )
     tgt_cells, tgt_pot, tgt_logw = (

time: 448 us -> 377 us (0.84)
  local copies, waits for them, and re-layouts: 49.1 us -> 13 us
  blocking collectives: 287 us -> 265 us
  matrix products: 51 us -> 32.4 us
  starting transfers between devices: 0.04 us -> 7.51 us
    all_gather x1 -> x0, blocking collectives: 23.8 us -> none  [body(): lax.all_gather(source, 'tgt', axis=1, tiled=True)]
    dynamic_update_slice x34, local copies, waits for them, and re-layouts: 22.7 us -> 1.3 us  [log_sums(): result = lax.map(one_block, blocks)]
    dot_general x17, matrix products: 40.6 us -> 25.1 us  [cost_scores(): lax.dot_general(row_cells, col_cells, (((0,), (0,)), ((), ())), precision...]
    dynamic_slice x13, local copies, waits for them, and re-layouts: 11.9 us -> 0.29 us  [log_sums(): result = lax.map(one_block, blocks)]
    all_to_all x0 -> x1, starting transfers between devices: none -> 7.48 us  [all_by_exchange(): blocks = lax.all_to_all(blocks, axis, split_axis=0, concat_axis=0)]
  transfers between devices with their start and end apart: 1 -> 2, of which waited for: 1 -> 1; matrix products, arithmetic and copies ran while one was open for 1% -> 2% of each run, Pallas kernels for 0% -> 0%
where the time goes in v1:
time: 377 us; the launch traced here: 376 us
  blocking collectives  265 us (70%)
  waiting for transfers between devices  34.2 us (9%)
  matrix products  32.4 us (9%)
  between operations  16.2 us (4%)
  local copies, waits for them, and re-layouts  13 us (3%)
  other arithmetic  7.6 us (2%)
  starting transfers between devices  7.51 us (2%)
    unnamed x2, blocking collectives  83.4 us
    psum x1, blocking collectives, body(): row_totals = lax.psum(row_totals * jnp.exp(row_top - highest), 'tgt')  40.4 us
    pmax x1, blocking collectives, body(): highest = lax.pmax(row_top, 'tgt')  36.3 us
    pmax x1, blocking collectives, body(): proj_highest = lax.pmax(proj_top, 'tgt')  35.5 us
    unnamed x2, waiting for transfers between devices  34.2 us
    dot_general x17, matrix products, cost_scores(): lax.dot_general(row_cells, col_cells, (((0,), (0,)), ((), ())), precision...  25.1 us
    psum x1, blocking collectives, body(): col_totals = lax.psum(col_totals * jnp.exp(col_top - col_highest), 'src')  24.2 us
    pmax x1, blocking collectives, body(): col_highest = lax.pmax(col_top, 'src')  24.1 us
  transfers between devices with their start and end apart: 2, of which 1 were waited for; matrix products, arithmetic and copies ran while one was open for 2% of the time, Pallas kernels for 0%

profile of v1, /device:TPU:2, one launch (start us, length us, event | category | flops | bytes accessed | tf_op | source)
XLA Modules:
  0.0 376.2 jit_solution(175652257653016064)
XLA Ops:
  7.2 0.7 stack.2
  7.9 0.8 reshape.86
  8.7 7.5 %all-to-all-start = ((f32[16,1,2048]{2,1,0:T(1,128)}), f32[16,1,2048]{2,1,0:T(1,128)S(1)}, u32[]{:S(2)}, u32[]{:S(2)}) async-start(f32[16,1,2048]{2,1,0:T(1,128)} %reshape.86), calls=%async_computation | async-start | bytes 262144 | tf_op jit(solution)/shard_map/all_to_all | solution.py:14
  16.3 20.9 %all-gather = f32[16,104,32]{1,2,0:T(8,128)S(1)} all-gather(f32[1,104,32]{1,2,0:T(8,128)} %bitcast.123), channel_id=1, replica_groups=mesh['src'=16,'tgt'=16] {'src'}, dimensions={0}, use_global_device_ids=true | all-gather | bytes 226304 | tf_op jit(solution)/shard_map/all_gather | solution.py:67
  37.2 1.3 dynamic-slice
  39.1 0.9 dynamic-update-slice
  40.0 0.9 dynamic-update-slice.1
  40.8 45.9 %all-reduce.5 = (f32[1664]{0:T(1024)S(1)}, f32[1664]{0:T(1024)S(1)}) all-reduce(f32[1664]{0:T(1024)S(1)} %dynamic-update-slice, f32[1664]{0:T(1024)S(1)} %dynamic-update-slice.1), channel_id=1, replica_groups=mesh['src'=16,'tgt'=16] {'src'}, use_global_device_ids=true, to_apply=%add | all-reduce | flops 3328 | bytes 26624
  87.1 1.4 fusion.21
  89.2 0.9 dynamic-update-slice.2
  90.1 0.5 broadcast.57
  90.6 0.9 reduce.1
  91.7 0.2 copy.21
  92.3 8.9 %while.38 = (s32[]{:T(128)}, f32[2,512]{1,0:T(2,128)S(1)}, f32[2,512]{1,0:T(2,128)S(1)}, f32[1664]{0:T(1024)S(1)}, f32[2,32,512]{2,1,0:T(8,128)S(1)}, /*index=5*...) while((s32[]{:T(128)}, f32[2,512]{1,0:T(2,128)S(1)}, ...), condition=%wide.region_5.6_spmd, body=%wide.region_1.5_spmd.sunk | while | flops 334854656 | bytes 7202941 | solution.py:52
  92.3 3.7 fusion.41
  96.0 0.6 exponential_reduce_fusion.4
  96.7 3.7 fusion.41
  100.5 0.6 exponential_reduce_fusion.4
  101.2 36.3 %pmax.21 = f32[1024]{0:T(1024)S(1)} all-reduce(f32[1024]{0:T(1024)S(1)} %bitcast.119), channel_id=1, replica_groups=mesh['src'=16,'tgt'=16] {'tgt'}, use_global_device_ids=true, to_apply=%region_6.7 | all-reduce | flops 1024 | bytes 8192 | tf_op jit(solution)/shard_map/pmax | solution.py:72
  137.5 40.4 %all-reduce.4 = (f32[1024]{0:T(1024)S(1)}, f32[1024]{0:T(1024)S(1)}) all-reduce(f32[1024]{0:T(1024)S(1)} %exponential_multiply_fusion, f32[1024]{0:T(1024)S(1)} %dynamic-update-slice.2), channel_id=1, replica_groups=mesh['src'=16,'tgt'=16] {'tgt'}, use_global_device_ids=true, to_apply=%region_7.8 | all-reduce | flops 2048 | bytes 16384 | tf_op jit(solution)/shard_map/psum | solution.py:73
  178.0 15.3 %while.39 = (s32[]{:T(128)}, f32[13,128]{1,0:T(8,128)S(1)}, f32[13,128]{1,0:T(8,128)S(1)}, f32[1024]{0:T(1024)S(1)}, f32[13,32,128]{2,0,1:T(8,128)S(1)}, /*index...) while((s32[]{:T(128)}, f32[13,128]{1,0:T(8,128)S(1)}, ...), condition=%wide.region_13.14_spmd, body=%wide.region_9.13_spmd.sunk | while | flops 51519104 | bytes 1262201 | solution.py:52
  178.0 0.8 fusion.44
  178.8 0.2 exponential_reduce_fusion.5
  179.2 0.8 fusion.44
  180.0 0.2 exponential_reduce_fusion.5
  180.4 0.8 fusion.44
  181.2 0.2 exponential_reduce_fusion.5
  181.5 0.8 fusion.44
  182.3 0.2 exponential_reduce_fusion.5
  182.7 0.8 fusion.44
  183.5 0.2 exponential_reduce_fusion.5
  183.9 0.8 fusion.44
  184.7 0.2 exponential_reduce_fusion.5
  185.1 0.8 fusion.44
  185.9 0.2 exponential_reduce_fusion.5
  186.2 0.8 fusion.44
  187.0 0.2 exponential_reduce_fusion.5
  187.4 0.8 fusion.44
  188.2 0.2 exponential_reduce_fusion.5
  188.6 0.8 fusion.44
  189.4 0.2 exponential_reduce_fusion.5
  189.8 0.8 fusion.44
  190.6 0.2 exponential_reduce_fusion.5
  191.0 0.8 fusion.44
  191.7 0.2 exponential_reduce_fusion.5
  192.1 0.8 fusion.44
  192.9 0.2 exponential_reduce_fusion.5
  193.2 24.1 %pmax.22 = f32[1664]{0:T(1024)S(1)} all-reduce(f32[1664]{0:T(1024)S(1)} %bitcast.122), channel_id=1, replica_groups=mesh['src'=16,'tgt'=16] {'src'}, use_global_device_ids=true, to_apply=%region_14.15 | all-reduce | flops 1664 | bytes 13312 | tf_op jit(solution)/shard_map/pmax | solution.py:77
  217.3 24.2 %psum.15 = f32[1664]{0:T(1024)S(1)} all-reduce(f32[1664]{0:T(1024)S(1)} %bitcast_multiply_fusion.2), channel_id=1, replica_groups=mesh['src'=16,'tgt'=16] {'src'}, use_global_device_ids=true, to_apply=%region_15.16 | all-reduce | flops 1664 | bytes 13312 | tf_op jit(solution)/shard_map/psum | solution.py:78
  241.6 16.2 %while.40 = (s32[]{:T(128)}, f32[2,512]{1,0:T(2,128)S(1)}, f32[2,512]{1,0:T(2,128)S(1)}, f32[2,32,512]{2,1,0:T(8,128)S(1)}, f32[1664]{0:T(1024)S(1)}, /*index=5*...) while((s32[]{:T(128)}, f32[2,512]{1,0:T(2,128)S(1)}, ...), condition=%wide.region_20.21_spmd, body=%wide.region_16.20_spmd.sunk | while | flops 662862336 | bytes 10891401 | solution.py:52
  241.6 3.7 fusion.48
  245.4 0.6 fusion.49
  246.0 3.6 fusion.50
  249.7 3.7 fusion.48
  253.4 0.6 fusion.49
  254.1 3.6 fusion.50
  257.8 35.5 %pmax.23 = f32[1024]{0:T(1024)S(1)} all-reduce(f32[1024]{0:T(1024)S(1)} %bitcast.117), channel_id=1, replica_groups=mesh['src'=16,'tgt'=16] {'tgt'}, use_global_device_ids=true, to_apply=%region_21.22 | all-reduce | flops 1024 | bytes 8192 | tf_op jit(solution)/shard_map/pmax | solution.py:86
  293.3 1.0 copy.28
  295.0 0.6 dynamic_slice.17
  295.6 0.6 dynamic_slice.18
  296.2 37.5 %all-reduce.3 = f32[1024]{0:T(1024)S(1)} all-reduce(f32[1024]{0:T(1024)S(1)} %get-tuple-element.274), channel_id=3, replica_groups=mesh['src'=16,'tgt'=16] {'tgt'}, use_global_device_ids=true, to_apply=%region_23.24.clone | all-reduce | flops 1024 | bytes 8192
  333.7 34.2 %reduce-scatter.4.cloned.1.call-done = f32[64,32]{1,0:T(8,128)} async-done(((f32[1024,32]{1,0:T(8,128)}), f32[64,32]{1,0:T(8,128)}) %reduce-scatter.4.cloned.1.call-update) | async-done | bytes 8208
  367.9 0.8 copy.29
  368.7 0.6 broadcast_divide_fusion
  (99 shorter events, 3.1 us)
Async XLA Ops:
  8.7 81.3 %all-to-all-start = ((f32[16,1,2048]{2,1,0:T(1,128)}), f32[16,1,2048]{2,1,0:T(1,128)S(1)}, u32[]{:S(2)}, u32[]{:S(2)}) async-start(f32[16,1,2048]{2,1,0:T(1,128)} %reshape.86), calls=%async_computation | async-start | bytes 262144 | tf_op jit(solution)/shard_map/all_to_all | solution.py:14
  16.2 351.7 %reduce-scatter.4.cloned.1.call-start = ((), (), s32[]{:S(2)}) async-start(), calls=%async_computation.2 | async-start | bytes 557056
Sparse Core Ops, SparseCore 0:
  294.5 73.3 reduce-scatter.3
